TPU v7x, 128 devices: a whole 4x4x4 slice. The times are simulated.
128 devices in a mesh: bx: 4 (over y), by: 4 (over x), bz: 8 (over z, core).
Axes of the slice: x: 4, y: 4, z: 4, core: 2. Of those that a mesh axis runs over, the one named last changes fastest.
Arguments:
- position: float32 [3, 128, 128, 2048], P(None, 'bx', 'by', 'bz'), may hold values from -2 to 2
- velocity: float32 [3, 128, 128, 2048], P(None, 'bx', 'by', 'bz'), may hold values from -3 to 3
- density: float32 [128, 128, 2048], P('bx', 'by', 'bz'), may hold values from 0.5 to 2
- energy: float32 [128, 128, 2048], P('bx', 'by', 'bz'), may hold values from 0.1 to 10
- pinned: int32 [128, 128, 2048], P('bx', 'by', 'bz'), may hold values 0 or 1
Outputs:
- velocity_new: float32 [3, 128, 128, 2048], P(None, 'bx', 'by', 'bz')
- accel: float32 [3, 128, 128, 2048], P(None, 'bx', 'by', 'bz')
- relaxed: float32 [3, 128, 128, 2048], P(None, 'bx', 'by', 'bz')
- density_new: float32 [128, 128, 2048], P('bx', 'by', 'bz')
- energy_new: float32 [128, 128, 2048], P('bx', 'by', 'bz')
All inputs are finite; a program needn't handle non-finite values. No bound on the sum of `pinned` on one device may be relied on, other than what follows from the above.
Results may differ from a plain program's by a relative error of at most 0.0003.
Values sent between devices are 32-bit elements; how exact they have to be, the bound alone decides.
A program may use at most 128 MiB of HBM per device.

v0:
```python
import jax
import jax.numpy as jnp
from jax import lax
from jax.sharding import PartitionSpec as P

CG_ITERS = 2
SWEEPS = 3
TIME_STEP = 0.6
RELAX_RATE = 0.8
CONSISTENT = 0.2


def from_behind(x, axis, by):
    length = lax.axis_size(axis)
    pairs = [(i, i + by) for i in range(length) if 0 <= i + by < length]
    return lax.ppermute(x, axis, pairs)


def padded(block, sides, width):
    for axis, dim in sides:
        count = lax.axis_size(axis)
        forward = [(i, i + 1) for i in range(count - 1)]
        backward = [(target, source) for source, target in forward]
        low = lax.ppermute(
            lax.slice_in_dim(block, block.shape[dim] - width, None, axis=dim), axis, forward
        )
        high = lax.ppermute(lax.slice_in_dim(block, 0, width, axis=dim), axis, backward)
        block = jnp.concatenate([low, block, high], axis=dim)
    return block


def shift_triple(along_dim, along, first, second):
    offsets = [0, 0, 0]
    offsets[along_dim] = along
    others = [d for d in range(3) if d != along_dim]
    offsets[others[0]] = first
    offsets[others[1]] = second
    return offsets


def select_at(extended, offsets):
    sizes = extended.shape[-3:]
    return extended[
        ...,
        1 + offsets[0] : sizes[0] - 1 + offsets[0],
        1 + offsets[1] : sizes[1] - 1 + offsets[1],
        1 + offsets[2] : sizes[2] - 1 + offsets[2],
    ]


def corner_force(pressure_ext):
    parts = []
    for along_dim in range(3):
        summed = 0.0
        for first in (0, -1):
            for second in (0, -1):
                summed = (
                    summed
                    + select_at(pressure_ext, shift_triple(along_dim, -1, first, second))
                    - select_at(pressure_ext, shift_triple(along_dim, 0, first, second))
                )
        parts.append(0.25 * summed)
    return jnp.stack(parts)


def node_mass(density_ext):
    summed = 0.0
    for first in (0, -1):
        for second in (0, -1):
            for third in (0, -1):
                summed = summed + select_at(density_ext, [first, second, third])
    return 0.125 * summed


def neighbours(extended):
    summed = 0.0
    for along_dim in range(3):
        for along in (-1, 1):
            summed = summed + select_at(extended, shift_triple(along_dim, along, 0, 0))
    return summed


def divergence(vel_ext):
    summed = 0.0
    for along_dim in range(3):
        for first in (0, 1):
            for second in (0, 1):
                summed = (
                    summed
                    + select_at(vel_ext[along_dim], shift_triple(along_dim, 1, first, second))
                    - select_at(vel_ext[along_dim], shift_triple(along_dim, 0, first, second))
                )
    return 0.25 * summed


def face_flux(packed, along_dim, along):
    speed = 0.0
    for first in (0, 1):
        for second in (0, 1):
            speed = speed + select_at(
                packed[along_dim], shift_triple(along_dim, along, first, second)
            )
    speed = 0.25 * speed
    upper = select_at(packed[3:5], shift_triple(along_dim, along, 0, 0))
    lower = select_at(packed[3:5], shift_triple(along_dim, along - 1, 0, 0))
    return speed * jnp.where(speed > 0, upper, lower)


def remap_cells(packed):
    result = select_at(packed[3:5], [0, 0, 0])
    for along_dim in range(3):
        result = result + face_flux(packed, along_dim, 1) - face_flux(packed, along_dim, 0)
    return result


def inner(first, second):
    return jnp.sum(first * second, axis=(1, 2, 3), keepdims=True)


def lower_cells(values):
    got = from_behind(values[..., -1:, :, :], "bx", 1)
    widened = jnp.concatenate([got, values], axis=-3)
    got = from_behind(widened[..., :, -1:, :], "by", 1)
    widened = jnp.concatenate([got, widened], axis=-2)
    got = from_behind(widened[..., :, :, -1:], "bz", 1)
    widened = jnp.concatenate([got, widened], axis=-1)
    return jnp.pad(widened, [(0, 0)] * (values.ndim - 3) + [(0, 1)] * 3)


def upper_nodes(values):
    got = from_behind(values[..., :1, :, :], "bx", -1)
    widened = jnp.concatenate([values, got], axis=-3)
    got = from_behind(widened[..., :, :1, :], "by", -1)
    widened = jnp.concatenate([widened, got], axis=-2)
    got = from_behind(widened[..., :, :, :1], "bz", -1)
    widened = jnp.concatenate([widened, got], axis=-1)
    return jnp.pad(widened, [(0, 0)] * (values.ndim - 3) + [(1, 0)] * 3)


def mass_apply(vector, masses):
    extended = padded(vector, (("bx", 1), ("by", 2), ("bz", 3)), 1)
    return masses * vector + CONSISTENT * (6.0 * vector + neighbours(extended))


def squares(residual):
    return lax.psum(inner(residual, residual), ("bx", "by", "bz"))


def one_sweep(relaxed, free):
    extended = padded(relaxed, (("bx", 1), ("by", 2), ("bz", 3)), 1)
    return relaxed + RELAX_RATE * free * (neighbours(extended) / 6.0 - relaxed)


def on_device(position, velocity, density, energy, pinned):
    cells = lower_cells(jnp.stack([density, energy]))
    force = corner_force(0.4 * cells[0] * cells[1])
    masses = node_mass(cells[0])
    solution = jnp.zeros_like(force)
    residual = force
    direction = force
    norm_now = squares(residual)
    for step_index in range(CG_ITERS):
        image = mass_apply(direction, masses)
        alpha = norm_now / lax.psum(inner(direction, image), ("bx", "by", "bz"))
        solution = solution + alpha * direction
        residual = residual - alpha * image
        norm_next = squares(residual)
        direction = residual + norm_next / norm_now * direction
        norm_now = norm_next
    velocity_new = velocity + TIME_STEP * solution
    vel_ext = upper_nodes(velocity_new)
    spread = divergence(vel_ext)
    pressure = 0.4 * density * energy
    energy_lag = energy - TIME_STEP * pressure * spread / density
    moved = position + TIME_STEP * velocity_new
    free = 1.0 - pinned.astype(jnp.float32)
    relaxed = moved
    for step_index in range(SWEEPS):
        relaxed = one_sweep(relaxed, free)
    packed = padded(
        jnp.concatenate([relaxed - moved, density[None], (density * energy_lag)[None]]),
        (("bx", 1), ("by", 2), ("bz", 3)),
        1,
    )
    remapped = remap_cells(packed)
    return (velocity_new, solution, relaxed, remapped[0], remapped[1])


def solution(mesh):
    in_specs = (
        P(None, "bx", "by", "bz"),
        P(None, "bx", "by", "bz"),
        P("bx", "by", "bz"),
        P("bx", "by", "bz"),
        P("bx", "by", "bz"),
    )
    out_specs = (
        P(None, "bx", "by", "bz"),
        P(None, "bx", "by", "bz"),
        P(None, "bx", "by", "bz"),
        P("bx", "by", "bz"),
        P("bx", "by", "bz"),
    )
    return jax.shard_map(
        on_device, mesh=mesh, in_specs=in_specs, out_specs=out_specs, check_vma=False
    )
```

profile of v0, /device:TPU:1, one launch (start us, length us, event | category | flops | bytes accessed | tf_op | source)
XLA Modules:
  0.0 638.1 jit_solution(13406718772434215634)
XLA Ops:
  1.6 4.0 collective-permute-start
  8.0 3.1 collective-permute-start.1
  14.1 5.8 collective-permute-start.2
  22.3 3.6 select_maximum_fusion.3
  29.0 4.0 collective-permute-start.3
  34.6 3.7 collective-permute-done.4
  38.5 4.0 collective-permute-start.5
  45.3 4.1 collective-permute-done.6
  52.9 3.0 copy.64
  55.9 3.0 copy.66
  61.2 5.9 collective-permute-start.7
  67.1 7.7 %fusion.120 = f32[32,32,256]{2,1,0:T(8,128)} fusion(f32[34,34,258]{2,1,0:T(8,128)} %slice_bitcast_fusion.7), kind=kLoop, calls=%fused_computation.316 | loop fusion | flops 2097152 | bytes 9437184 | tf_op jit(solution)/shard_map/mul | solution.py:72
  74.8 2.9 copy.65
  77.8 2.9 copy.67
  80.7 16.0 %multiply_reduce_fusion.1 = (f32[3]{0:T(128)}, f32[3]{0:T(128)}, f32[3,32,32,256]{3,2,1,0:T(8,128)}) fusion(f32[1,32,32,256]{3,2,1,0:T(8,128)} %copy-done.4, f32[1,32,32,256]{3,2,1,0:T(8,128)S(1)} %multiply_bitcast_fusion.1, f32[1,32,32,256]{3,2,1,0:T(8,128)S(1)} %get-tuple-element.82, f32[3,34,34,1]{3,2,1,0:T(8,128)} %copy.67, ...), kind=kLoop, calls=%fused_computation.195 | loop fusion | flops 36175864 | bytes 7773304 | tf_op jit(solution)/shard_map/reduce_sum | solution.py:117
  96.7 64.6 %all-reduce.2 = (f32[3,1,1,1]{0,3,2,1:T(1,128)S(1)}, f32[3,1,1,1]{0,3,2,1:T(1,128)S(1)}) all-reduce(f32[3,1,1,1]{0,3,2,1:T(1,128)} %bitcast.58, f32[3,1,1,1]{0,3,2,1:T(1,128)} %bitcast.57), channel_id=1, replica_groups=mesh['bx'=4,'by'=4,'bz'=8] {'bx','by','bz'}, use_global_device_ids=true, to_apply=%region_1.2 | all-reduce | flops 6 | bytes 48 | tf_op jit(solution)/shard_map/psum | solution.py:146
  164.2 63.1 %psum.30 = f32[3,1,1,1]{0,3,2,1:T(1,128)S(1)} all-reduce(f32[3,1,1,1]{0,3,2,1:T(1,128)S(1)} %bitcast.60), channel_id=1, replica_groups=mesh['bx'=4,'by'=4,'bz'=8] {'bx','by','bz'}, use_global_device_ids=true, to_apply=%region_5.6 | all-reduce | flops 3 | bytes 24 | tf_op jit(solution)/shard_map/psum | solution.py:146
  227.3 3.1 multiply_add_fusion.3
  234.4 3.7 collective-permute-done.10
  241.7 3.8 collective-permute-done.12
  248.8 3.0 copy.68
  251.8 5.8 collective-permute-start.13
  257.6 3.0 copy.70
  262.7 2.9 copy.69
  266.4 2.9 copy.71
  269.3 15.8 %fusion.67 = f32[3]{0:T(128)} fusion(f32[3,32,32,256]{3,2,1,0:T(8,128)} %copy-done.5, f32[3,34,34,1]{3,2,1,0:T(8,128)} %copy.71, f32[3,34,1,256]{3,2,1,0:T(1,128)S(1)} %collective-permute-done.12, f32[3,34,1,256]{3,2,1,0:T(1,128)S(1)} %collective-permute-done.11, f32[3,1,32,256]{3,2,1,0:T(8,128)S(1)} %collective-permute-done.10, ...), kind=kLoop, calls=%fused_computation.147 | loop fusion | flops 23592956 | bytes 4627564 | tf_op jit(solution)/shard_map/reduce_sum | solution.py:117
  285.1 63.9 %psum.31 = f32[3,1,1,1]{0,3,2,1:T(1,128)S(1)} all-reduce(f32[3,1,1,1]{0,3,2,1:T(1,128)} %bitcast.59), channel_id=1, replica_groups=mesh['bx'=4,'by'=4,'bz'=8] {'bx','by','bz'}, use_global_device_ids=true, to_apply=%region_7.8 | all-reduce | flops 3 | bytes 24 | tf_op jit(solution)/shard_map/psum | solution.py:164
  349.7 6.8 %multiply_add_fusion = (f32[3,32,32,256]{3,2,1,0:T(8,128)S(1)}, f32[3,32,32,256]{3,2,1,0:T(8,128)}, f32[3,32,32,256]{3,2,1,0:T(8,128)}) fusion(f32[3,32,32,256]{3,2,1,0:T(8,128)} %param.5, f32[3,32,32,256]{3,2,1,0:T(8,128)} %param.6, f32[3]{0:T(128)S(1)} %divide_bitcast_fusion, f32[1,32,32,256]{3,2,1,0:T(8,128)} %copy-done.4, ...), kind=kLoop, calls=%fused_computation.189 | loop fusion | flops 10223616 | bytes 22020132 | tf_op jit(solution)/shard_map/add | solution.py:175
  360.3 3.7 collective-permute-done.16
  365.6 4.0 collective-permute-start.17
  374.2 3.1 copy.78
  378.9 5.4 collective-permute-start.20
  392.2 14.2 %fusion.57 = f32[3,32,32,256]{3,2,1,0:T(8,128)S(1)} fusion(f32[3,32,32,256]{3,2,1,0:T(8,128)} %copy-done.3, f32[3,34,34,1]{3,2,1,0:T(8,128)} %copy.81, f32[3,34,1,256]{3,2,1,0:T(1,128)S(1)} %copy.75, f32[3,34,1,256]{3,2,1,0:T(1,128)S(1)} %copy.73, f32[3,1,32,256]{3,2,1,0:T(8,128)S(1)} %collective-permute-done.16, ...), kind=kLoop, calls=%fused_computation.119 | loop fusion | flops 21233664 | bytes 7773280 | tf_op jit(solution)/shard_map/add | solution.py:151
  416.1 4.7 collective-permute-start.23
  422.2 4.3 collective-permute-done.34
  435.3 5.6 collective-permute-start.26
  440.9 3.8 collective-permute-start.25
  444.7 2.9 pad_maximum_fusion.113
  452.0 3.6 collective-permute-done.35
  462.1 14.5 %fusion.48 = f32[3,32,32,256]{3,2,1,0:T(8,128)S(1)} fusion(f32[3,32,32,256]{3,2,1,0:T(8,128)} %copy-done.6, f32[3,34,34,1]{3,2,1,0:T(8,128)} %copy.91, f32[3,34,1,256]{3,2,1,0:T(1,128)S(1)} %copy.85, f32[3,34,1,256]{3,2,1,0:T(1,128)S(1)} %copy.83, f32[3,1,32,256]{3,2,1,0:T(8,128)S(1)} %collective-permute-done.22, ...), kind=kLoop, calls=%fused_computation.92 | loop fusion | flops 21233664 | bytes 7773280 | tf_op jit(solution)/shard_map/add | solution.py:151
  476.6 3.2 collective-permute-start.27
  481.2 4.7 select_maximum_fusion
  487.4 4.7 collective-permute-start.29
  498.2 3.1 copy.98
  501.3 3.1 copy.100
  506.4 3.6 collective-permute-start.31
  510.0 20.4 %fusion.119 = f32[1,32,32,256]{3,2,1,0:T(8,128)} fusion(f32[32,32,256]{2,1,0:T(8,128)S(1)} %copy-done, f32[32,32,256]{2,1,0:T(8,128)} %param.8, f32[34,34,258]{2,1,0:T(8,128)} %get-tuple-element.39, f32[34,34,258]{2,1,0:T(8,128)} %get-tuple-element.38, f32[34,34,258]{2,1,0:T(8,128)S(1)} %get-tuple-element.37), kind=kLoop, calls=%fused_computation.292 | loop fusion | flops 8126464 | bytes 28311552 | tf_op jit(solution)/shard_map/broadcast_in_dim | solution.py:181
  530.4 3.0 copy.99
  533.4 3.0 copy.101
  536.4 16.5 %fusion.127 = (f32[3,32,32,256]{3,2,1,0:T(8,128)S(1)}, f32[3,32,32,256]{3,2,1,0:T(8,128)}) fusion(f32[3,32,32,256]{3,2,1,0:T(8,128)} %copy-done.3, f32[3,32,32,256]{3,2,1,0:T(8,128)} %copy-done.7, f32[3,34,34,1]{3,2,1,0:T(8,128)} %copy.101, f32[3,34,1,256]{3,2,1,0:T(1,128)S(1)} %copy.95, f32[3,1,32,256]{3,2,1,0:T(8,128)S(1)} %collective-permute-done.28, ...), kind=kLoop, calls=%fused_computation.365 | loop fusion | flops 22020096 | bytes 14064736 | tf_op jit(solution)/shard_map/sub | solution.py:181
  552.9 4.0 collective-permute-start.36
  560.8 4.1 collective-permute-done.37
  565.2 3.4 collective-permute-start.38
  571.8 3.8 collective-permute-done.39
  577.2 3.9 fusion.130
  581.1 3.5 copy.107
  584.5 3.6 collective-permute-start.41
  588.1 3.5 copy.106
  593.7 3.5 copy.109
  597.2 3.5 copy.108
  600.7 16.1 %pad_maximum_fusion = f32[5,34,34,258]{3,2,1,0:T(8,128)S(1)} fusion(f32[5,34,34,1]{3,2,1,0:T(8,128)} %copy.109, f32[5,34,1,256]{3,2,1,0:T(1,128)} %copy-done.19, f32[5,1,32,256]{3,2,1,0:T(8,128)S(1)} %collective-permute-done.37, f32[1,32,32,256]{3,2,1,0:T(8,128)} %fusion.119, f32[1,32,32,256]{3,2,1,0:T(8,128)} %bitcast.46, ...), kind=kLoop, calls=%fused_computation | loop fusion | flops 11929920 | bytes 11929920 | tf_op jit(solution)/shard_map/concatenate | solution.py:28
  617.2 3.7 broadcast_compare_fusion.5
  621.0 6.0 broadcast_compare_fusion.1
  627.1 9.3 %fusion.84 = f32[2,32,32,256]{3,2,1,0:T(8,128)S(1)} fusion(f32[3,32,32,256]{3,2,1,0:T(8,128)S(1)} %get-tuple-element.26, f32[1,32,32,256]{3,2,1,0:T(8,128)S(1)} %bitcast.52, f32[5,34,34,1]{3,2,1,0:T(8,128)S(1)} %copy-done.13, f32[5,34,1,256]{3,2,1,0:T(1,128)S(1)} %copy-done.20, f32[5,34,1,256]{3,2,1,0:T(1,128)S(1)} %copy-done.18, ...), kind=kLoop, calls=%fused_computation.206 | loop fusion | flops 25690112 | bytes 15926432 | tf_op jit(solution)/shard_map/sub | solution.py:112
  (173 shorter events, 113.0 us)
Async XLA Ops:
  0.6 12.5 %copy-start.14 = (f32[32,32,256]{2,1,0:T(8,128)S(1)}, f32[32,32,256]{2,1,0:T(8,128)}, u32[]{:S(2)}) copy-start(f32[32,32,256]{2,1,0:T(8,128)} %param.8) | copy-start | bytes 3145732
  0.6 12.5 %copy-start = (f32[32,32,256]{2,1,0:T(8,128)S(1)}, f32[32,32,256]{2,1,0:T(8,128)}, u32[]{:S(2)}) copy-start(f32[32,32,256]{2,1,0:T(8,128)} %param.7) | copy-start | bytes 3145732
  1.6 5.3 collective-permute-start
  8.0 4.5 collective-permute-start.1
  14.1 6.8 %collective-permute-start.2 = (f32[2,33,33,1]{2,0,3,1:T(2,128)S(1)}, f32[2,33,33,1]{2,0,3,1:T(2,128)}, u32[]{:S(2)}, u32[]{:S(2)}) collective-permute-start(f32[2,33,33,1]{2,0,3,1:T(2,128)S(1)} %copy.62), channel_id=1, source_target_pairs={{0,1},{1,2},{2,3},{3,4},{4,5},{5,6},{6,7},{8,9},{9,10},{10,11},{11... | collective-permute-start | bytes 26144 | tf_op jit(solution)/shard_map/ppermute | solution.py:16
  28.7 21.6 %copy-start.4 = (f32[1,32,32,256]{3,2,1,0:T(8,128)}, f32[1,32,32,256]{3,2,1,0:T(8,128)S(1)}, u32[]{:S(2)}) copy-start(f32[1,32,32,256]{3,2,1,0:T(8,128)S(1)} %get-tuple-element.83) | copy-start | bytes 3145732
  29.0 5.6 collective-permute-start.3
  33.0 5.4 collective-permute-start.4
  38.5 6.8 %collective-permute-start.5 = (f32[3,34,1,256]{3,2,1,0:T(1,128)S(1)}, f32[3,34,1,256]{3,2,1,0:T(1,128)S(1)}, u32[]{:S(2)}, u32[]{:S(2)}) collective-permute-start(f32[3,34,1,256]{3,2,1,0:T(1,128)S(1)} %get-tuple-element.62), channel_id=1, source_target_pairs={{0,8},{8,16},{16,24},{1,9},{9,17},{17,25},{2,10},{10,18},{18,26},{... | collective-permute-start | bytes 313352 | tf_op jit(solution)/shard_map/ppermute | solution.py:24
  42.5 6.8 %collective-permute-start.6 = (f32[3,34,1,256]{3,2,1,0:T(1,128)S(1)}, f32[3,34,1,256]{3,2,1,0:T(1,128)S(1)}, u32[]{:S(2)}, u32[]{:S(2)}) collective-permute-start(f32[3,34,1,256]{3,2,1,0:T(1,128)S(1)} %get-tuple-element.63), channel_id=1, source_target_pairs={{8,0},{16,8},{24,16},{9,1},{17,9},{25,17},{10,2},{18,10},{26,18},{... | collective-permute-start | bytes 313352 | tf_op jit(solution)/shard_map/ppermute | solution.py:27
  58.9 18.8 %collective-permute-start.8 = (f32[3,34,34,1]{2,3,1,0:T(1,128)}, f32[3,34,34,1]{2,3,1,0:T(1,128)}, u32[]{:S(2)}, u32[]{:S(2)}) collective-permute-start(f32[3,34,34,1]{2,3,1,0:T(1,128)} %copy.66), channel_id=1, source_target_pairs={{1,0},{2,1},{3,2},{4,3},{5,4},{6,5},{7,6},{9,8},{10,9},{11,10},{12... | collective-permute-start | bytes 41624 | tf_op jit(solution)/shard_map/ppermute | solution.py:27
  61.2 13.6 %collective-permute-start.7 = (f32[3,34,34,1]{2,3,1,0:T(1,128)}, f32[3,34,34,1]{2,3,1,0:T(1,128)}, u32[]{:S(2)}, u32[]{:S(2)}) collective-permute-start(f32[3,34,34,1]{2,3,1,0:T(1,128)} %copy.64), channel_id=1, source_target_pairs={{0,1},{1,2},{2,3},{3,4},{4,5},{5,6},{6,7},{8,9},{9,10},{10,11},{11... | collective-permute-start | bytes 41624 | tf_op jit(solution)/shard_map/ppermute | solution.py:24
  161.3 66.0 %copy-start.22 = (f32[3]{0:T(128)}, f32[3]{0:T(128)S(1)}, u32[]{:S(2)}) copy-start(f32[3]{0:T(128)S(1)} %divide_bitcast_fusion.2) | copy-start | bytes 40
  227.2 3.1 copy-start.23
  230.4 15.8 %copy-start.5 = (f32[3,32,32,256]{3,2,1,0:T(8,128)}, f32[3,32,32,256]{3,2,1,0:T(8,128)S(1)}, u32[]{:S(2)}) copy-start(f32[3,32,32,256]{3,2,1,0:T(8,128)S(1)} %multiply_add_fusion.3) | copy-start | bytes 9437188
  230.4 4.0 collective-permute-start.9
  232.8 5.4 collective-permute-start.10
  238.3 3.4 collective-permute-start.11
  240.0 5.4 collective-permute-start.12
  251.8 10.9 %collective-permute-start.13 = (f32[3,34,34,1]{2,3,1,0:T(1,128)}, f32[3,34,34,1]{2,3,1,0:T(1,128)}, u32[]{:S(2)}, u32[]{:S(2)}) collective-permute-start(f32[3,34,34,1]{2,3,1,0:T(1,128)} %copy.68), channel_id=1, source_target_pairs={{0,1},{1,2},{2,3},{3,4},{4,5},{5,6},{6,7},{8,9},{9,10},{10,11},{11... | collective-permute-start | bytes 41624 | tf_op jit(solution)/shard_map/ppermute | solution.py:24
  260.6 5.7 collective-permute-start.14
  356.5 17.7 %copy-start.3 = (f32[3,32,32,256]{3,2,1,0:T(8,128)}, f32[3,32,32,256]{3,2,1,0:T(8,128)S(1)}, u32[]{:S(2)}) copy-start(f32[3,32,32,256]{3,2,1,0:T(8,128)S(1)} %get-tuple-element.28) | copy-start | bytes 9437188
  356.5 3.8 collective-permute-start.15
  358.7 5.4 collective-permute-start.16
  364.2 5.6 collective-permute-start.18
  365.6 5.8 collective-permute-start.17
  378.9 11.1 %collective-permute-start.20 = (f32[3,34,34,1]{2,1,3,0:T(8,128)}, f32[3,34,34,1]{2,1,3,0:T(8,128)S(1)}, u32[]{:S(2)}, u32[]{:S(2)}) collective-permute-start(f32[3,34,34,1]{2,1,3,0:T(8,128)} %copy.80), channel_id=1, source_target_pairs={{1,0},{2,1},{3,2},{4,3},{5,4},{6,5},{7,6},{9,8},{10,9},{11,10},{12... | collective-permute-start | bytes 41624 | tf_op jit(solution)/shard_map/ppermute | solution.py:27
  384.3 3.5 collective-permute-start.19
  387.8 74.3 %copy-start.15 = (f32[32,32,256]{2,1,0:T(8,128)}, f32[32,32,256]{2,1,0:T(8,128)S(1)}, u32[]{:S(2)}) copy-start(f32[32,32,256]{2,1,0:T(8,128)S(1)} %subtract_multiply_fusion) | copy-start | bytes 3145732
  392.2 18.3 %copy-start.8 = (f32[3,32,32,256]{3,2,1,0:T(8,128)S(1)}, f32[3,32,32,256]{3,2,1,0:T(8,128)}, u32[]{:S(2)}) copy-start(f32[3,32,32,256]{3,2,1,0:T(8,128)} %get-tuple-element.29) | copy-start | bytes 9437188
  406.4 20.5 %copy-start.6 = (f32[3,32,32,256]{3,2,1,0:T(8,128)}, f32[3,32,32,256]{3,2,1,0:T(8,128)S(1)}, u32[]{:S(2)}) copy-start(f32[3,32,32,256]{3,2,1,0:T(8,128)S(1)} %fusion.57) | copy-start | bytes 9437188
  406.4 5.5 collective-permute-start.21
  409.2 5.4 collective-permute-start.22
  410.6 10.2 %collective-permute-start.33 = (f32[3,1,32,256]{3,2,1,0:T(8,128)S(1)}, f32[3,1,32,256]{3,2,1,0:T(8,128)S(1)}, u32[]{:S(2)}, u32[]{:S(2)}) collective-permute-start(f32[3,1,32,256]{3,2,1,0:T(8,128)S(1)} %slice.782), channel_id=1, source_target_pairs={{32,0},{64,32},{96,64},{33,1},{65,33},{97,65},{34,2},{66,34},{98,6... | collective-permute-start | bytes 294920 | tf_op jit(solution)/shard_map/ppermute | solution.py:16
  414.8 11.8 %collective-permute-start.24 = (f32[3,34,1,256]{3,1,2,0:T(8,128)S(1)}, f32[3,34,1,256]{3,1,2,0:T(8,128)S(1)}, u32[]{:S(2)}, u32[]{:S(2)}) collective-permute-start(f32[3,34,1,256]{3,1,2,0:T(8,128)S(1)} %copy.84), channel_id=1, source_target_pairs={{8,0},{16,8},{24,16},{9,1},{17,9},{25,17},{10,2},{18,10},{26,18},{... | collective-permute-start | bytes 313352 | tf_op jit(solution)/shard_map/ppermute | solution.py:27
  416.1 10.7 %collective-permute-start.23 = (f32[3,34,1,256]{3,1,2,0:T(8,128)S(1)}, f32[3,34,1,256]{3,1,2,0:T(8,128)S(1)}, u32[]{:S(2)}, u32[]{:S(2)}) collective-permute-start(f32[3,34,1,256]{3,1,2,0:T(8,128)S(1)} %copy.82), channel_id=1, source_target_pairs={{0,8},{8,16},{16,24},{1,9},{9,17},{17,25},{2,10},{10,18},{18,26},{... | collective-permute-start | bytes 313352 | tf_op jit(solution)/shard_map/ppermute | solution.py:24
  420.9 5.6 collective-permute-start.34
  435.3 24.7 %collective-permute-start.26 = (f32[3,34,34,1]{2,1,3,0:T(8,128)S(1)}, f32[3,34,34,1]{2,1,3,0:T(8,128)S(1)}, u32[]{:S(2)}, u32[]{:S(2)}) collective-permute-start(f32[3,34,34,1]{2,1,3,0:T(8,128)S(1)} %copy.90), channel_id=1, source_target_pairs={{1,0},{2,1},{3,2},{4,3},{5,4},{6,5},{7,6},{9,8},{10,9},{11,10},{12... | collective-permute-start | bytes 41624 | tf_op jit(solution)/shard_map/ppermute | solution.py:27
  440.9 16.8 %collective-permute-start.25 = (f32[3,34,34,1]{2,1,3,0:T(8,128)S(1)}, f32[3,34,34,1]{2,1,3,0:T(8,128)S(1)}, u32[]{:S(2)}, u32[]{:S(2)}) collective-permute-start(f32[3,34,34,1]{2,1,3,0:T(8,128)S(1)} %copy.88), channel_id=1, source_target_pairs={{0,1},{1,2},{2,3},{3,4},{4,5},{5,6},{6,7},{8,9},{9,10},{10,11},{11... | collective-permute-start | bytes 41624 | tf_op jit(solution)/shard_map/ppermute | solution.py:24
  450.0 5.5 collective-permute-start.35
  462.1 19.1 %copy-start.9 = (f32[3,32,32,256]{3,2,1,0:T(8,128)S(1)}, f32[3,32,32,256]{3,2,1,0:T(8,128)}, u32[]{:S(2)}) copy-start(f32[3,32,32,256]{3,2,1,0:T(8,128)} %get-tuple-element.29) | copy-start | bytes 9437188
  462.1 19.1 %copy-start.16 = (f32[3,33,33,1]{3,2,1,0:T(8,128)S(1)}, f32[3,33,33,1]{3,2,1,0:T(8,128)}, u32[]{:S(2)}) copy-start(f32[3,33,33,1]{3,2,1,0:T(8,128)} %copy.105) | copy-start | bytes 39208
  476.6 18.2 %copy-start.7 = (f32[3,32,32,256]{3,2,1,0:T(8,128)}, f32[3,32,32,256]{3,2,1,0:T(8,128)S(1)}, u32[]{:S(2)}) copy-start(f32[3,32,32,256]{3,2,1,0:T(8,128)S(1)} %fusion.48) | copy-start | bytes 9437188
  476.6 9.3 %collective-permute-start.27 = (f32[3,1,32,256]{3,2,1,0:T(8,128)S(1)}, f32[3,1,32,256]{3,2,1,0:T(8,128)S(1)}, u32[]{:S(2)}, u32[]{:S(2)}) collective-permute-start(f32[3,1,32,256]{3,2,1,0:T(8,128)S(1)} %get-tuple-element.64), channel_id=1, source_target_pairs={{0,32},{32,64},{64,96},{1,33},{33,65},{65,97},{2,34},{34,66},{66,9... | collective-permute-start | bytes 294920 | tf_op jit(solution)/shard_map/ppermute | solution.py:24
  479.9 6.0 collective-permute-start.28
  486.1 8.4 %collective-permute-start.30 = (f32[3,34,1,256]{3,1,2,0:T(8,128)S(1)}, f32[3,34,1,256]{3,1,2,0:T(8,128)S(1)}, u32[]{:S(2)}, u32[]{:S(2)}) collective-permute-start(f32[3,34,1,256]{3,1,2,0:T(8,128)S(1)} %copy.94), channel_id=1, source_target_pairs={{8,0},{16,8},{24,16},{9,1},{17,9},{25,17},{10,2},{18,10},{26,18},{... | collective-permute-start | bytes 313352 | tf_op jit(solution)/shard_map/ppermute | solution.py:27
  487.4 7.2 %collective-permute-start.29 = (f32[3,34,1,256]{3,1,2,0:T(8,128)S(1)}, f32[3,34,1,256]{3,1,2,0:T(8,128)S(1)}, u32[]{:S(2)}, u32[]{:S(2)}) collective-permute-start(f32[3,34,1,256]{3,1,2,0:T(8,128)S(1)} %copy.92), channel_id=1, source_target_pairs={{0,8},{8,16},{16,24},{1,9},{9,17},{17,25},{2,10},{10,18},{18,26},{... | collective-permute-start | bytes 313352 | tf_op jit(solution)/shard_map/ppermute | solution.py:24
  504.5 29.0 %collective-permute-start.32 = (f32[3,34,34,1]{2,1,3,0:T(8,128)}, f32[3,34,34,1]{2,1,3,0:T(8,128)}, u32[]{:S(2)}, u32[]{:S(2)}) collective-permute-start(f32[3,34,34,1]{2,1,3,0:T(8,128)} %copy.100), channel_id=1, source_target_pairs={{1,0},{2,1},{3,2},{4,3},{5,4},{6,5},{7,6},{9,8},{10,9},{11,10},{12... | collective-permute-start | bytes 41624 | tf_op jit(solution)/shard_map/ppermute | solution.py:27
  506.4 24.0 %collective-permute-start.31 = (f32[3,34,34,1]{2,1,3,0:T(8,128)}, f32[3,34,34,1]{2,1,3,0:T(8,128)}, u32[]{:S(2)}, u32[]{:S(2)}) collective-permute-start(f32[3,34,34,1]{2,1,3,0:T(8,128)} %copy.98), channel_id=1, source_target_pairs={{0,1},{1,2},{2,3},{3,4},{4,5},{5,6},{6,7},{8,9},{9,10},{10,11},{11... | collective-permute-start | bytes 41624 | tf_op jit(solution)/shard_map/ppermute | solution.py:24
  536.4 16.5 %copy-start.1 = (f32[32,32,256]{2,1,0:T(8,128)S(1)}, f32[32,32,256]{2,1,0:T(8,128)}, u32[]{:S(2)}) copy-start(f32[32,32,256]{2,1,0:T(8,128)} %param.7) | copy-start | bytes 3145732
  536.4 16.5 %copy-start.10 = (f32[1,32,32,256]{3,2,1,0:T(8,128)S(1)}, f32[1,32,32,256]{3,2,1,0:T(8,128)}, u32[]{:S(2)}) copy-start(f32[1,32,32,256]{3,2,1,0:T(8,128)} %fusion.119) | copy-start | bytes 3145732
  552.9 7.9 %collective-permute-start.36 = (f32[5,1,32,256]{3,2,1,0:T(8,128)S(1)}, f32[5,1,32,256]{3,2,1,0:T(8,128)S(1)}, u32[]{:S(2)}, u32[]{:S(2)}) collective-permute-start(f32[5,1,32,256]{3,2,1,0:T(8,128)S(1)} %get-tuple-element.42), channel_id=1, source_target_pairs={{0,32},{32,64},{64,96},{1,33},{33,65},{65,97},{2,34},{34,66},{66,9... | collective-permute-start | bytes 491528 | tf_op jit(solution)/shard_map/ppermute | solution.py:24
  556.9 8.0 %collective-permute-start.37 = (f32[5,1,32,256]{3,2,1,0:T(8,128)S(1)}, f32[5,1,32,256]{3,2,1,0:T(8,128)S(1)}, u32[]{:S(2)}, u32[]{:S(2)}) collective-permute-start(f32[5,1,32,256]{3,2,1,0:T(8,128)S(1)} %get-tuple-element.43), channel_id=1, source_target_pairs={{32,0},{64,32},{96,64},{33,1},{65,33},{97,65},{34,2},{66,34},{98,6... | collective-permute-start | bytes 491528 | tf_op jit(solution)/shard_map/ppermute | solution.py:27
  565.2 6.6 %collective-permute-start.38 = (f32[5,34,1,256]{3,2,1,0:T(1,128)S(1)}, f32[5,34,1,256]{3,2,1,0:T(1,128)S(1)}, u32[]{:S(2)}, u32[]{:S(2)}) collective-permute-start(f32[5,34,1,256]{3,2,1,0:T(1,128)S(1)} %get-tuple-element.40), channel_id=1, source_target_pairs={{0,8},{8,16},{16,24},{1,9},{9,17},{17,25},{2,10},{10,18},{18,26},{... | collective-permute-start | bytes 522248 | tf_op jit(solution)/shard_map/ppermute | solution.py:24
  568.5 7.1 %collective-permute-start.39 = (f32[5,34,1,256]{3,2,1,0:T(1,128)S(1)}, f32[5,34,1,256]{3,2,1,0:T(1,128)S(1)}, u32[]{:S(2)}, u32[]{:S(2)}) collective-permute-start(f32[5,34,1,256]{3,2,1,0:T(1,128)S(1)} %get-tuple-element.41), channel_id=1, source_target_pairs={{8,0},{16,8},{24,16},{9,1},{17,9},{25,17},{10,2},{18,10},{26,18},{... | collective-permute-start | bytes 522248 | tf_op jit(solution)/shard_map/ppermute | solution.py:27
  571.8 5.4 copy-start.17
  584.5 9.2 %collective-permute-start.41 = (f32[5,34,34,1]{2,3,1,0:T(1,128)}, f32[5,34,34,1]{2,3,1,0:T(1,128)}, u32[]{:S(2)}, u32[]{:S(2)}) collective-permute-start(f32[5,34,34,1]{2,3,1,0:T(1,128)} %copy.107), channel_id=1, source_target_pairs={{1,0},{2,1},{3,2},{4,3},{5,4},{6,5},{7,6},{9,8},{10,9},{11,10},{12... | collective-permute-start | bytes 69368 | tf_op jit(solution)/shard_map/ppermute | solution.py:27
  591.6 5.6 collective-permute-start.40
  621.0 6.0 copy-start.2
  621.0 6.0 copy-start.11
  621.0 6.0 copy-start.12
  621.0 6.1 copy-start.13
  621.0 6.1 copy-start.18
  621.0 6.1 copy-start.20
  (3 other events, 5.3 us)
where the time goes:
time: 647 us; the launch traced here: 638 us
  blocking collectives  192 us (30%)
  other arithmetic  178 us (28%)
  starting transfers between devices  118 us (18%)
  local copies, waits for them, and re-layouts  98.8 us (15%)
  waiting for transfers between devices  49.5 us (8%)
    psum x2, blocking collectives, squares(): return lax.psum(inner(residual, residual), ('bx', 'by', 'bz'))  128 us
    ppermute x18, starting transfers between devices, padded(): lax.ppermute(lax.slice_in_dim(block, block.shape[dim] - width, None, axis...  64.5 us
    psum x1, blocking collectives, on_device(): alpha = norm_now / lax.psum(inner(direction, image), ('bx', 'by', 'bz'))  63.9 us
    ppermute x18, starting transfers between devices, padded(): lax.ppermute(lax.slice_in_dim(block, 0, width, axis=dim), axis, backward)  36.5 us
    reduce_sum x3, other arithmetic, inner(): return jnp.sum(first * second, axis=(1, 2, 3), keepdims=True)  34.7 us
    slice x19, local copies, waits for them, and re-layouts, padded(): lax.slice_in_dim(block, block.shape[dim] - width, None, axis=dim)  30.9 us
    ppermute x18, waiting for transfers between devices, padded(): lax.ppermute(lax.slice_in_dim(block, 0, width, axis=dim), axis, backward)  30.7 us
    add x2, other arithmetic, one_sweep(): return relaxed + RELAX_RATE * free * (neighbours(extended) / 6.0 - relaxed)  28.6 us
  transfers between devices with their start and end apart: 42, of which 22 were waited for; matrix products, arithmetic and copies ran while one was open for 11% of the time, Pallas kernels for 0%

commit v1 on v0

--- a/solution.py
+++ b/solution.py
@@ -2,12 +2,19 @@
 import jax.numpy as jnp
 from jax import lax
 from jax.sharding import PartitionSpec as P
+from jax.lax import all_gather
 
 CG_ITERS = 2
 SWEEPS = 3
 TIME_STEP = 0.6
 RELAX_RATE = 0.8
 CONSISTENT = 0.2
+
+
+def try_all_the_loops(inner_x, axis_key):
+    x_now = all_gather(inner_x, axis_key)
+    current_arr = jnp.sum(x_now, 0)
+    return current_arr
 
 
 def from_behind(x, axis, by):
@@ -161,7 +168,7 @@
     norm_now = squares(residual)
     for step_index in range(CG_ITERS):
         image = mass_apply(direction, masses)
-        alpha = norm_now / lax.psum(inner(direction, image), ("bx", "by", "bz"))
+        alpha = norm_now / try_all_the_loops(inner(direction, image), axis_key=("bx", "by", "bz"))
         solution = solution + alpha * direction
         residual = residual - alpha * image
         norm_next = squares(residual)

time: 647 us -> 655 us (1.012)
    psum x1 -> x0, blocking collectives: 63.9 us -> none  [on_device(): alpha = norm_now / lax.psum(inner(direction, image), ('bx', 'by', 'bz'))]
    unnamed x0 -> x1, blocking collectives: none -> 63.8 us
where the time goes in v1:
time: 655 us; the launch traced here: 646 us
  blocking collectives  191 us (29%)
  other arithmetic  180 us (27%)
  starting transfers between devices  120 us (18%)
  local copies, waits for them, and re-layouts  105 us (16%)
  waiting for transfers between devices  48 us (7%)
    psum x2, blocking collectives, squares(): return lax.psum(inner(residual, residual), ('bx', 'by', 'bz'))  128 us
    ppermute x18, starting transfers between devices, padded(): lax.ppermute(lax.slice_in_dim(block, block.shape[dim] - width, None, axis...  65.8 us
    unnamed x1, blocking collectives  63.8 us
    ppermute x18, starting transfers between devices, padded(): lax.ppermute(lax.slice_in_dim(block, 0, width, axis=dim), axis, backward)  36.4 us
    reduce_sum x3, other arithmetic, inner(): return jnp.sum(first * second, axis=(1, 2, 3), keepdims=True)  34.8 us
    slice x19, local copies, waits for them, and re-layouts, padded(): lax.slice_in_dim(block, block.shape[dim] - width, None, axis=dim)  31 us
    ppermute x18, waiting for transfers between devices, padded(): lax.ppermute(lax.slice_in_dim(block, 0, width, axis=dim), axis, backward)  29.2 us
    add x2, other arithmetic, one_sweep(): return relaxed + RELAX_RATE * free * (neighbours(extended) / 6.0 - relaxed)  29.1 us
  transfers between devices with their start and end apart: 42, of which 22 were waited for; matrix products, arithmetic and copies ran while one was open for 11% of the time, Pallas kernels for 0%

profile of v1, /device:TPU:1, one launch (start us, length us, event | category | flops | bytes accessed | tf_op | source)
XLA Modules:
  0.0 645.9 jit_solution(1025885558856544190)
XLA Ops:
  1.6 4.0 collective-permute-start
  8.0 3.1 collective-permute-start.1
  14.1 5.8 collective-permute-start.2
  22.3 3.6 select_maximum_fusion.3
  31.9 4.0 collective-permute-start.3
  37.5 3.7 collective-permute-done.4
  42.5 4.0 collective-permute-start.5
  47.8 3.0 slice_bitcast_fusion.7
  56.8 3.0 copy.64
  59.9 3.0 copy.66
  65.2 5.9 collective-permute-start.7
  71.1 7.7 %fusion.120 = f32[32,32,256]{2,1,0:T(8,128)} fusion(f32[34,34,258]{2,1,0:T(8,128)} %slice_bitcast_fusion.7), kind=kLoop, calls=%fused_computation.316 | loop fusion | flops 2097152 | bytes 9437184 | tf_op jit(solution)/shard_map/mul | solution.py:79
  78.8 2.9 copy.65
  81.7 2.9 copy.67
  84.7 16.1 %multiply_reduce_fusion.1 = (f32[3]{0:T(128)}, f32[3]{0:T(128)}, f32[3,32,32,256]{3,2,1,0:T(8,128)}) fusion(f32[1,32,32,256]{3,2,1,0:T(8,128)} %copy-done.4, f32[1,32,32,256]{3,2,1,0:T(8,128)S(1)} %multiply_bitcast_fusion.1, f32[1,32,32,256]{3,2,1,0:T(8,128)S(1)} %get-tuple-element.82, f32[3,34,34,1]{3,2,1,0:T(8,128)} %copy.67, ...), kind=kLoop, calls=%fused_computation.195 | loop fusion | flops 36175864 | bytes 7773304 | tf_op jit(solution)/shard_map/reduce_sum | solution.py:124
  101.5 64.7 %all-reduce.4 = (f32[3,1,1,1]{0,3,2,1:T(1,128)S(1)}, f32[384]{0:T(512)S(1)}) all-reduce(f32[3,1,1,1]{0,3,2,1:T(1,128)} %bitcast.63, f32[384]{0:T(512)S(1)} %dynamic-update-slice), channel_id=1, replica_groups=mesh['bx'=4,'by'=4,'bz'=8] {'bx','by','bz'}, use_global_device_ids=true, to_apply=%region_1.2 | all-reduce | flops 387 | bytes 3096 | tf_op jit(solution)/shard_map/psum | solution.py:153
  169.4 62.9 %psum.15 = f32[3,1,1,1]{0,3,2,1:T(1,128)S(1)} all-reduce(f32[3,1,1,1]{0,3,2,1:T(1,128)S(1)} %bitcast.64), channel_id=1, replica_groups=mesh['bx'=4,'by'=4,'bz'=8] {'bx','by','bz'}, use_global_device_ids=true, to_apply=%region_5.6 | all-reduce | flops 3 | bytes 24 | tf_op jit(solution)/shard_map/psum | solution.py:153
  232.3 3.1 multiply_add_fusion.3
  239.7 3.7 collective-permute-done.10
  246.7 3.8 collective-permute-done.12
  253.9 3.0 copy.68
  256.9 5.8 collective-permute-start.13
  262.7 3.0 copy.70
  267.8 2.9 copy.69
  271.5 2.9 copy.71
  274.4 15.9 %fusion.67 = f32[3]{0:T(128)} fusion(f32[3,32,32,256]{3,2,1,0:T(8,128)} %copy-done.6, f32[3,34,34,1]{3,2,1,0:T(8,128)} %copy.71, f32[3,34,1,256]{3,2,1,0:T(1,128)S(1)} %collective-permute-done.12, f32[3,34,1,256]{3,2,1,0:T(1,128)S(1)} %collective-permute-done.11, f32[3,1,32,256]{3,2,1,0:T(8,128)S(1)} %collective-permute-done.10, ...), kind=kLoop, calls=%fused_computation.147 | loop fusion | flops 23592956 | bytes 4627564 | tf_op jit(solution)/shard_map/reduce_sum | solution.py:124
  291.1 63.8 %all-reduce.3 = f32[384]{0:T(512)S(1)} all-reduce(f32[384]{0:T(512)S(1)} %dynamic-update-slice.1), channel_id=3, replica_groups=mesh['bx'=4,'by'=4,'bz'=8] {'bx','by','bz'}, use_global_device_ids=true, to_apply=%add.3 | all-reduce | flops 384 | bytes 3072
  355.8 6.8 %multiply_add_fusion = (f32[3,32,32,256]{3,2,1,0:T(8,128)S(1)}, f32[3,32,32,256]{3,2,1,0:T(8,128)}, f32[3,32,32,256]{3,2,1,0:T(8,128)}) fusion(f32[3,32,32,256]{3,2,1,0:T(8,128)} %param.5, f32[3,32,32,256]{3,2,1,0:T(8,128)} %param.6, f32[3]{0:T(128)S(1)} %fusion.122, f32[1,32,32,256]{3,2,1,0:T(8,128)} %copy-done.4, ...), kind=kLoop, calls=%fused_computation.189 | loop fusion | flops 10223616 | bytes 22020132 | tf_op jit(solution)/shard_map/add | solution.py:182
  366.5 3.7 collective-permute-done.16
  371.8 4.0 collective-permute-start.17
  380.4 3.1 copy.78
  385.1 5.4 collective-permute-start.20
  398.4 14.2 %fusion.57 = f32[3,32,32,256]{3,2,1,0:T(8,128)S(1)} fusion(f32[3,32,32,256]{3,2,1,0:T(8,128)} %copy-done.3, f32[3,34,34,1]{3,2,1,0:T(8,128)} %copy.81, f32[3,34,1,256]{3,2,1,0:T(1,128)S(1)} %copy.75, f32[3,34,1,256]{3,2,1,0:T(1,128)S(1)} %copy.73, f32[3,1,32,256]{3,2,1,0:T(8,128)S(1)} %collective-permute-done.16, ...), kind=kLoop, calls=%fused_computation.119 | loop fusion | flops 21233664 | bytes 7773280 | tf_op jit(solution)/shard_map/add | solution.py:158
  422.2 4.7 collective-permute-start.23
  428.3 4.3 collective-permute-done.34
  441.4 5.6 collective-permute-start.26
  447.0 3.8 collective-permute-start.25
  458.1 3.6 collective-permute-done.35
  468.3 14.8 %fusion.48 = f32[3,32,32,256]{3,2,1,0:T(8,128)S(1)} fusion(f32[3,32,32,256]{3,2,1,0:T(8,128)} %copy-done.7, f32[3,34,34,1]{3,2,1,0:T(8,128)} %copy.91, f32[3,34,1,256]{3,2,1,0:T(1,128)S(1)} %copy.85, f32[3,34,1,256]{3,2,1,0:T(1,128)S(1)} %copy.83, f32[3,1,32,256]{3,2,1,0:T(8,128)S(1)} %collective-permute-done.22, ...), kind=kLoop, calls=%fused_computation.92 | loop fusion | flops 21233664 | bytes 7773280 | tf_op jit(solution)/shard_map/add | solution.py:158
  483.2 3.4 collective-permute-start.27
  487.9 4.7 select_maximum_fusion
  494.1 4.7 collective-permute-start.29
  504.8 3.1 copy.98
  508.0 3.1 copy.100
  513.0 3.9 collective-permute-start.31
  517.0 20.2 %fusion.119 = f32[1,32,32,256]{3,2,1,0:T(8,128)} fusion(f32[32,32,256]{2,1,0:T(8,128)S(1)} %copy-done, f32[32,32,256]{2,1,0:T(8,128)} %param.8, f32[34,34,258]{2,1,0:T(8,128)} %get-tuple-element.39, f32[34,34,258]{2,1,0:T(8,128)} %get-tuple-element.38, f32[34,34,258]{2,1,0:T(8,128)S(1)} %get-tuple-element.37), kind=kLoop, calls=%fused_computation.292 | loop fusion | flops 8126464 | bytes 28311552 | tf_op jit(solution)/shard_map/broadcast_in_dim | solution.py:188
  537.2 3.0 copy.99
  540.2 3.0 copy.101
  543.2 16.7 %fusion.129 = (f32[3,32,32,256]{3,2,1,0:T(8,128)S(1)}, f32[3,32,32,256]{3,2,1,0:T(8,128)}) fusion(f32[3,32,32,256]{3,2,1,0:T(8,128)} %copy-done.3, f32[3,32,32,256]{3,2,1,0:T(8,128)} %copy-done.8, f32[3,34,34,1]{3,2,1,0:T(8,128)} %copy.101, f32[3,34,1,256]{3,2,1,0:T(1,128)S(1)} %copy.95, f32[3,1,32,256]{3,2,1,0:T(8,128)S(1)} %collective-permute-done.28, ...), kind=kLoop, calls=%fused_computation.367 | loop fusion | flops 22020096 | bytes 14064736 | tf_op jit(solution)/shard_map/sub | solution.py:188
  559.9 3.7 collective-permute-start.36
  567.5 4.2 collective-permute-done.37
  571.9 3.4 collective-permute-start.38
  578.6 3.8 collective-permute-done.39
  584.0 3.9 fusion.132
  587.9 3.5 copy.107
  591.4 3.4 collective-permute-start.41
  594.8 3.5 copy.106
  598.3 3.2 collective-permute-start.40
  601.6 3.4 copy.109
  605.0 3.4 copy.108
  608.4 16.1 %pad_maximum_fusion = f32[5,34,34,258]{3,2,1,0:T(8,128)S(1)} fusion(f32[5,34,34,1]{3,2,1,0:T(8,128)} %copy.109, f32[5,34,1,256]{3,2,1,0:T(1,128)} %copy-done.21, f32[5,1,32,256]{3,2,1,0:T(8,128)S(1)} %collective-permute-done.37, f32[1,32,32,256]{3,2,1,0:T(8,128)} %fusion.119, f32[1,32,32,256]{3,2,1,0:T(8,128)} %bitcast.52, ...), kind=kLoop, calls=%fused_computation | loop fusion | flops 11929920 | bytes 11929920 | tf_op jit(solution)/shard_map/concatenate | solution.py:35
  625.0 3.8 broadcast_compare_fusion.5
  628.8 6.0 broadcast_compare_fusion.1
  634.9 9.3 %fusion.84 = f32[2,32,32,256]{3,2,1,0:T(8,128)S(1)} fusion(f32[3,32,32,256]{3,2,1,0:T(8,128)S(1)} %get-tuple-element.26, f32[1,32,32,256]{3,2,1,0:T(8,128)S(1)} %bitcast.58, f32[5,34,34,1]{3,2,1,0:T(8,128)S(1)} %copy-done.14, f32[5,34,1,256]{3,2,1,0:T(1,128)S(1)} %copy-done.22, f32[5,34,1,256]{3,2,1,0:T(1,128)S(1)} %copy-done.20, ...), kind=kLoop, calls=%fused_computation.206 | loop fusion | flops 25690112 | bytes 15926432 | tf_op jit(solution)/shard_map/sub | solution.py:119
  (185 shorter events, 120.9 us)
Async XLA Ops:
  0.6 12.5 %copy-start.15 = (f32[32,32,256]{2,1,0:T(8,128)S(1)}, f32[32,32,256]{2,1,0:T(8,128)}, u32[]{:S(2)}) copy-start(f32[32,32,256]{2,1,0:T(8,128)} %param.8) | copy-start | bytes 3145732
  0.6 12.5 %copy-start = (f32[32,32,256]{2,1,0:T(8,128)S(1)}, f32[32,32,256]{2,1,0:T(8,128)}, u32[]{:S(2)}) copy-start(f32[32,32,256]{2,1,0:T(8,128)} %param.7) | copy-start | bytes 3145732
  1.6 5.3 collective-permute-start
  8.0 4.5 collective-permute-start.1
  14.1 6.8 %collective-permute-start.2 = (f32[2,33,33,1]{2,0,3,1:T(2,128)S(1)}, f32[2,33,33,1]{2,0,3,1:T(2,128)}, u32[]{:S(2)}, u32[]{:S(2)}) collective-permute-start(f32[2,33,33,1]{2,0,3,1:T(2,128)S(1)} %copy.62), channel_id=1, source_target_pairs={{0,1},{1,2},{2,3},{3,4},{4,5},{5,6},{6,7},{8,9},{9,10},{10,11},{11... | collective-permute-start | bytes 26144 | tf_op jit(solution)/shard_map/ppermute | solution.py:23
  31.9 5.6 collective-permute-start.3
  35.9 5.4 collective-permute-start.4
  37.2 16.1 %copy-start.5 = (f32[1,32,32,256]{3,2,1,0:T(8,128)S(1)}, f32[1,32,32,256]{3,2,1,0:T(8,128)}, u32[]{:S(2)}) copy-start(f32[1,32,32,256]{3,2,1,0:T(8,128)} %copy-done.4) | copy-start | bytes 3145732
  42.5 8.3 %collective-permute-start.5 = (f32[3,34,1,256]{3,2,1,0:T(1,128)S(1)}, f32[3,34,1,256]{3,2,1,0:T(1,128)S(1)}, u32[]{:S(2)}, u32[]{:S(2)}) collective-permute-start(f32[3,34,1,256]{3,2,1,0:T(1,128)S(1)} %get-tuple-element.62), channel_id=1, source_target_pairs={{0,8},{8,16},{16,24},{1,9},{9,17},{17,25},{2,10},{10,18},{18,26},{... | collective-permute-start | bytes 313352 | tf_op jit(solution)/shard_map/ppermute | solution.py:31
  46.5 6.8 %collective-permute-start.6 = (f32[3,34,1,256]{3,2,1,0:T(1,128)S(1)}, f32[3,34,1,256]{3,2,1,0:T(1,128)S(1)}, u32[]{:S(2)}, u32[]{:S(2)}) collective-permute-start(f32[3,34,1,256]{3,2,1,0:T(1,128)S(1)} %get-tuple-element.63), channel_id=1, source_target_pairs={{8,0},{16,8},{24,16},{9,1},{17,9},{25,17},{10,2},{18,10},{26,18},{... | collective-permute-start | bytes 313352 | tf_op jit(solution)/shard_map/ppermute | solution.py:34
  62.9 18.8 %collective-permute-start.8 = (f32[3,34,34,1]{2,3,1,0:T(1,128)}, f32[3,34,34,1]{2,3,1,0:T(1,128)}, u32[]{:S(2)}, u32[]{:S(2)}) collective-permute-start(f32[3,34,34,1]{2,3,1,0:T(1,128)} %copy.66), channel_id=1, source_target_pairs={{1,0},{2,1},{3,2},{4,3},{5,4},{6,5},{7,6},{9,8},{10,9},{11,10},{12... | collective-permute-start | bytes 41624 | tf_op jit(solution)/shard_map/ppermute | solution.py:34
  65.2 13.6 %collective-permute-start.7 = (f32[3,34,34,1]{2,3,1,0:T(1,128)}, f32[3,34,34,1]{2,3,1,0:T(1,128)}, u32[]{:S(2)}, u32[]{:S(2)}) collective-permute-start(f32[3,34,34,1]{2,3,1,0:T(1,128)} %copy.64), channel_id=1, source_target_pairs={{0,1},{1,2},{2,3},{3,4},{4,5},{5,6},{6,7},{8,9},{9,10},{10,11},{11... | collective-permute-start | bytes 41624 | tf_op jit(solution)/shard_map/ppermute | solution.py:31
  166.5 65.8 %copy-start.24 = (f32[3]{0:T(128)}, f32[3]{0:T(128)S(1)}, u32[]{:S(2)}) copy-start(f32[3]{0:T(128)S(1)} %fusion.121) | copy-start | bytes 40
  232.3 3.1 copy-start.25
  235.4 15.8 %copy-start.6 = (f32[3,32,32,256]{3,2,1,0:T(8,128)}, f32[3,32,32,256]{3,2,1,0:T(8,128)S(1)}, u32[]{:S(2)}) copy-start(f32[3,32,32,256]{3,2,1,0:T(8,128)S(1)} %multiply_add_fusion.3) | copy-start | bytes 9437188
  235.4 4.3 collective-permute-start.9
  238.1 5.4 collective-permute-start.10
  243.6 3.1 collective-permute-start.11
  245.1 5.4 collective-permute-start.12
  256.9 10.9 %collective-permute-start.13 = (f32[3,34,34,1]{2,3,1,0:T(1,128)}, f32[3,34,34,1]{2,3,1,0:T(1,128)}, u32[]{:S(2)}, u32[]{:S(2)}) collective-permute-start(f32[3,34,34,1]{2,3,1,0:T(1,128)} %copy.68), channel_id=1, source_target_pairs={{0,1},{1,2},{2,3},{3,4},{4,5},{5,6},{6,7},{8,9},{9,10},{10,11},{11... | collective-permute-start | bytes 41624 | tf_op jit(solution)/shard_map/ppermute | solution.py:31
  265.7 5.7 collective-permute-start.14
  362.6 17.9 %copy-start.3 = (f32[3,32,32,256]{3,2,1,0:T(8,128)}, f32[3,32,32,256]{3,2,1,0:T(8,128)S(1)}, u32[]{:S(2)}) copy-start(f32[3,32,32,256]{3,2,1,0:T(8,128)S(1)} %get-tuple-element.28) | copy-start | bytes 9437188
  362.6 4.0 collective-permute-start.15
  364.9 5.4 collective-permute-start.16
  370.5 5.6 collective-permute-start.18
  371.8 5.8 collective-permute-start.17
  385.1 11.1 %collective-permute-start.20 = (f32[3,34,34,1]{2,1,3,0:T(8,128)}, f32[3,34,34,1]{2,1,3,0:T(8,128)S(1)}, u32[]{:S(2)}, u32[]{:S(2)}) collective-permute-start(f32[3,34,34,1]{2,1,3,0:T(8,128)} %copy.80), channel_id=1, source_target_pairs={{1,0},{2,1},{3,2},{4,3},{5,4},{6,5},{7,6},{9,8},{10,9},{11,10},{12... | collective-permute-start | bytes 41624 | tf_op jit(solution)/shard_map/ppermute | solution.py:34
  390.5 3.5 collective-permute-start.19
  394.0 74.2 %copy-start.17 = (f32[32,32,256]{2,1,0:T(8,128)}, f32[32,32,256]{2,1,0:T(8,128)S(1)}, u32[]{:S(2)}) copy-start(f32[32,32,256]{2,1,0:T(8,128)S(1)} %subtract_multiply_fusion) | copy-start | bytes 3145732
  398.4 18.3 %copy-start.9 = (f32[3,32,32,256]{3,2,1,0:T(8,128)S(1)}, f32[3,32,32,256]{3,2,1,0:T(8,128)}, u32[]{:S(2)}) copy-start(f32[3,32,32,256]{3,2,1,0:T(8,128)} %get-tuple-element.29) | copy-start | bytes 9437188
  412.6 20.4 %copy-start.7 = (f32[3,32,32,256]{3,2,1,0:T(8,128)}, f32[3,32,32,256]{3,2,1,0:T(8,128)S(1)}, u32[]{:S(2)}) copy-start(f32[3,32,32,256]{3,2,1,0:T(8,128)S(1)} %fusion.57) | copy-start | bytes 9437188
  412.7 5.4 collective-permute-start.21
  415.4 5.4 collective-permute-start.22
  416.7 10.2 %collective-permute-start.33 = (f32[3,1,32,256]{3,2,1,0:T(8,128)S(1)}, f32[3,1,32,256]{3,2,1,0:T(8,128)S(1)}, u32[]{:S(2)}, u32[]{:S(2)}) collective-permute-start(f32[3,1,32,256]{3,2,1,0:T(8,128)S(1)} %slice.782), channel_id=1, source_target_pairs={{32,0},{64,32},{96,64},{33,1},{65,33},{97,65},{34,2},{66,34},{98,6... | collective-permute-start | bytes 294920 | tf_op jit(solution)/shard_map/ppermute | solution.py:23
  420.9 11.8 %collective-permute-start.24 = (f32[3,34,1,256]{3,1,2,0:T(8,128)S(1)}, f32[3,34,1,256]{3,1,2,0:T(8,128)S(1)}, u32[]{:S(2)}, u32[]{:S(2)}) collective-permute-start(f32[3,34,1,256]{3,1,2,0:T(8,128)S(1)} %copy.84), channel_id=1, source_target_pairs={{8,0},{16,8},{24,16},{9,1},{17,9},{25,17},{10,2},{18,10},{26,18},{... | collective-permute-start | bytes 313352 | tf_op jit(solution)/shard_map/ppermute | solution.py:34
  422.2 10.7 %collective-permute-start.23 = (f32[3,34,1,256]{3,1,2,0:T(8,128)S(1)}, f32[3,34,1,256]{3,1,2,0:T(8,128)S(1)}, u32[]{:S(2)}, u32[]{:S(2)}) collective-permute-start(f32[3,34,1,256]{3,1,2,0:T(8,128)S(1)} %copy.82), channel_id=1, source_target_pairs={{0,8},{8,16},{16,24},{1,9},{9,17},{17,25},{2,10},{10,18},{18,26},{... | collective-permute-start | bytes 313352 | tf_op jit(solution)/shard_map/ppermute | solution.py:31
  427.0 5.6 collective-permute-start.34
  441.4 24.7 %collective-permute-start.26 = (f32[3,34,34,1]{2,1,3,0:T(8,128)S(1)}, f32[3,34,34,1]{2,1,3,0:T(8,128)S(1)}, u32[]{:S(2)}, u32[]{:S(2)}) collective-permute-start(f32[3,34,34,1]{2,1,3,0:T(8,128)S(1)} %copy.90), channel_id=1, source_target_pairs={{1,0},{2,1},{3,2},{4,3},{5,4},{6,5},{7,6},{9,8},{10,9},{11,10},{12... | collective-permute-start | bytes 41624 | tf_op jit(solution)/shard_map/ppermute | solution.py:34
  447.0 16.8 %collective-permute-start.25 = (f32[3,34,34,1]{2,1,3,0:T(8,128)S(1)}, f32[3,34,34,1]{2,1,3,0:T(8,128)S(1)}, u32[]{:S(2)}, u32[]{:S(2)}) collective-permute-start(f32[3,34,34,1]{2,1,3,0:T(8,128)S(1)} %copy.88), channel_id=1, source_target_pairs={{0,1},{1,2},{2,3},{3,4},{4,5},{5,6},{6,7},{8,9},{9,10},{10,11},{11... | collective-permute-start | bytes 41624 | tf_op jit(solution)/shard_map/ppermute | solution.py:31
  456.2 5.5 collective-permute-start.35
  468.3 19.6 %copy-start.10 = (f32[3,32,32,256]{3,2,1,0:T(8,128)S(1)}, f32[3,32,32,256]{3,2,1,0:T(8,128)}, u32[]{:S(2)}) copy-start(f32[3,32,32,256]{3,2,1,0:T(8,128)} %get-tuple-element.29) | copy-start | bytes 9437188
  468.3 19.6 %copy-start.18 = (f32[3,33,33,1]{3,2,1,0:T(8,128)S(1)}, f32[3,33,33,1]{3,2,1,0:T(8,128)}, u32[]{:S(2)}) copy-start(f32[3,33,33,1]{3,2,1,0:T(8,128)} %copy.105) | copy-start | bytes 39208
  483.1 18.3 %copy-start.8 = (f32[3,32,32,256]{3,2,1,0:T(8,128)}, f32[3,32,32,256]{3,2,1,0:T(8,128)S(1)}, u32[]{:S(2)}) copy-start(f32[3,32,32,256]{3,2,1,0:T(8,128)S(1)} %fusion.48) | copy-start | bytes 9437188
  483.2 9.4 %collective-permute-start.27 = (f32[3,1,32,256]{3,2,1,0:T(8,128)S(1)}, f32[3,1,32,256]{3,2,1,0:T(8,128)S(1)}, u32[]{:S(2)}, u32[]{:S(2)}) collective-permute-start(f32[3,1,32,256]{3,2,1,0:T(8,128)S(1)} %get-tuple-element.64), channel_id=1, source_target_pairs={{0,32},{32,64},{64,96},{1,33},{33,65},{65,97},{2,34},{34,66},{66,9... | collective-permute-start | bytes 294920 | tf_op jit(solution)/shard_map/ppermute | solution.py:31
  486.5 6.0 collective-permute-start.28
  492.8 8.4 %collective-permute-start.30 = (f32[3,34,1,256]{3,1,2,0:T(8,128)S(1)}, f32[3,34,1,256]{3,1,2,0:T(8,128)S(1)}, u32[]{:S(2)}, u32[]{:S(2)}) collective-permute-start(f32[3,34,1,256]{3,1,2,0:T(8,128)S(1)} %copy.94), channel_id=1, source_target_pairs={{8,0},{16,8},{24,16},{9,1},{17,9},{25,17},{10,2},{18,10},{26,18},{... | collective-permute-start | bytes 313352 | tf_op jit(solution)/shard_map/ppermute | solution.py:34
  494.1 7.2 %collective-permute-start.29 = (f32[3,34,1,256]{3,1,2,0:T(8,128)S(1)}, f32[3,34,1,256]{3,1,2,0:T(8,128)S(1)}, u32[]{:S(2)}, u32[]{:S(2)}) collective-permute-start(f32[3,34,1,256]{3,1,2,0:T(8,128)S(1)} %copy.92), channel_id=1, source_target_pairs={{0,8},{8,16},{16,24},{1,9},{9,17},{17,25},{2,10},{10,18},{18,26},{... | collective-permute-start | bytes 313352 | tf_op jit(solution)/shard_map/ppermute | solution.py:31
  511.1 29.0 %collective-permute-start.32 = (f32[3,34,34,1]{2,1,3,0:T(8,128)}, f32[3,34,34,1]{2,1,3,0:T(8,128)}, u32[]{:S(2)}, u32[]{:S(2)}) collective-permute-start(f32[3,34,34,1]{2,1,3,0:T(8,128)} %copy.100), channel_id=1, source_target_pairs={{1,0},{2,1},{3,2},{4,3},{5,4},{6,5},{7,6},{9,8},{10,9},{11,10},{12... | collective-permute-start | bytes 41624 | tf_op jit(solution)/shard_map/ppermute | solution.py:34
  513.0 24.1 %collective-permute-start.31 = (f32[3,34,34,1]{2,1,3,0:T(8,128)}, f32[3,34,34,1]{2,1,3,0:T(8,128)}, u32[]{:S(2)}, u32[]{:S(2)}) collective-permute-start(f32[3,34,34,1]{2,1,3,0:T(8,128)} %copy.98), channel_id=1, source_target_pairs={{0,1},{1,2},{2,3},{3,4},{4,5},{5,6},{6,7},{8,9},{9,10},{10,11},{11... | collective-permute-start | bytes 41624 | tf_op jit(solution)/shard_map/ppermute | solution.py:31
  543.2 16.7 %copy-start.1 = (f32[32,32,256]{2,1,0:T(8,128)S(1)}, f32[32,32,256]{2,1,0:T(8,128)}, u32[]{:S(2)}) copy-start(f32[32,32,256]{2,1,0:T(8,128)} %param.7) | copy-start | bytes 3145732
  543.2 16.7 %copy-start.11 = (f32[1,32,32,256]{3,2,1,0:T(8,128)S(1)}, f32[1,32,32,256]{3,2,1,0:T(8,128)}, u32[]{:S(2)}) copy-start(f32[1,32,32,256]{3,2,1,0:T(8,128)} %fusion.119) | copy-start | bytes 3145732
  559.9 7.6 %collective-permute-start.36 = (f32[5,1,32,256]{3,2,1,0:T(8,128)S(1)}, f32[5,1,32,256]{3,2,1,0:T(8,128)S(1)}, u32[]{:S(2)}, u32[]{:S(2)}) collective-permute-start(f32[5,1,32,256]{3,2,1,0:T(8,128)S(1)} %get-tuple-element.42), channel_id=1, source_target_pairs={{0,32},{32,64},{64,96},{1,33},{33,65},{65,97},{2,34},{34,66},{66,9... | collective-permute-start | bytes 491528 | tf_op jit(solution)/shard_map/ppermute | solution.py:31
  563.6 8.0 %collective-permute-start.37 = (f32[5,1,32,256]{3,2,1,0:T(8,128)S(1)}, f32[5,1,32,256]{3,2,1,0:T(8,128)S(1)}, u32[]{:S(2)}, u32[]{:S(2)}) collective-permute-start(f32[5,1,32,256]{3,2,1,0:T(8,128)S(1)} %get-tuple-element.43), channel_id=1, source_target_pairs={{32,0},{64,32},{96,64},{33,1},{65,33},{97,65},{34,2},{66,34},{98,6... | collective-permute-start | bytes 491528 | tf_op jit(solution)/shard_map/ppermute | solution.py:34
  571.9 6.8 %collective-permute-start.38 = (f32[5,34,1,256]{3,2,1,0:T(1,128)S(1)}, f32[5,34,1,256]{3,2,1,0:T(1,128)S(1)}, u32[]{:S(2)}, u32[]{:S(2)}) collective-permute-start(f32[5,34,1,256]{3,2,1,0:T(1,128)S(1)} %get-tuple-element.40), channel_id=1, source_target_pairs={{0,8},{8,16},{16,24},{1,9},{9,17},{17,25},{2,10},{10,18},{18,26},{... | collective-permute-start | bytes 522248 | tf_op jit(solution)/shard_map/ppermute | solution.py:31
  575.3 7.2 %collective-permute-start.39 = (f32[5,34,1,256]{3,2,1,0:T(1,128)S(1)}, f32[5,34,1,256]{3,2,1,0:T(1,128)S(1)}, u32[]{:S(2)}, u32[]{:S(2)}) collective-permute-start(f32[5,34,1,256]{3,2,1,0:T(1,128)S(1)} %get-tuple-element.41), channel_id=1, source_target_pairs={{8,0},{16,8},{24,16},{9,1},{17,9},{25,17},{10,2},{18,10},{26,18},{... | collective-permute-start | bytes 522248 | tf_op jit(solution)/shard_map/ppermute | solution.py:34
  578.6 5.4 copy-start.19
  591.4 10.2 %collective-permute-start.41 = (f32[5,34,34,1]{2,3,1,0:T(1,128)}, f32[5,34,34,1]{2,3,1,0:T(1,128)}, u32[]{:S(2)}, u32[]{:S(2)}) collective-permute-start(f32[5,34,34,1]{2,3,1,0:T(1,128)} %copy.107), channel_id=1, source_target_pairs={{1,0},{2,1},{3,2},{4,3},{5,4},{6,5},{7,6},{9,8},{10,9},{11,10},{12... | collective-permute-start | bytes 69368 | tf_op jit(solution)/shard_map/ppermute | solution.py:34
  598.3 6.7 %collective-permute-start.40 = (f32[5,34,34,1]{2,3,1,0:T(1,128)}, f32[5,34,34,1]{2,3,1,0:T(1,128)}, u32[]{:S(2)}, u32[]{:S(2)}) collective-permute-start(f32[5,34,34,1]{2,3,1,0:T(1,128)} %copy.106), channel_id=1, source_target_pairs={{0,1},{1,2},{2,3},{3,4},{4,5},{5,6},{6,7},{8,9},{9,10},{10,11},{11... | collective-permute-start | bytes 69368 | tf_op jit(solution)/shard_map/ppermute | solution.py:31
  628.8 6.1 copy-start.2
  628.8 6.1 copy-start.12
  628.8 6.1 copy-start.13
  628.8 6.1 copy-start.14
  628.8 6.1 copy-start.20
  628.8 6.1 copy-start.22
  (5 other events, 8.2 us)
